TPU v7x, 512 devices: a whole 4x4x16 slice. The times are simulated.
512 devices in a mesh: sect: 4 (over y), blk: 128 (over x, z, core).
Axes of the slice: x: 4, y: 4, z: 16, core: 2. Of those that a mesh axis runs over, the one named last changes fastest.
Arguments:
- site_tensor: bfloat16 [4, 6144, 1536], P('sect', 'blk'), may hold values from -0.5 to 0.5
- left_env: bfloat16 [4, 256, 384, 384], P('sect', 'blk'), may hold values from -0.23925781 to 0.23925781
- boundary_env: bfloat16 [256, 384, 384], P('blk'), may hold values from -6 to 6
- sector_sizes: int32 [16], replicated, may hold values from 110 to 384, as said below
- mpo_ops: float32 [16, 2, 4, 4], replicated, may hold values from -2 to 2
- mpo_mask: int32 [16, 2], replicated, may hold values 0 or 1
Outputs:
- envs: bfloat16 [4, 256, 384, 384], P('sect', 'blk')
- grads: bfloat16 [4, 6144, 1536], P('sect', 'blk')
Inputs may be any that keep to these rules, and one draw needn't show every extreme that they name: `sector_sizes`: exactly one sector holds 384 states, the others hold (1664) // 15 states or one more, and all sizes sum to 2048.
All inputs are finite; a program needn't handle non-finite values.
Results may differ from a plain program's by a relative error of at most 0.018.
Values may be sent and summed in bfloat16 or wider, within the bound.
A program may use at most 64 MiB of HBM per device.

v0:
```python
from functools import partial

import jax
import jax.numpy as jnp
from jax import lax
from jax.sharding import PartitionSpec as P

S = 16
W = 16
PHYS = 4
TILE = 128


CHARGE = (0, 1, 1, 2)
CLASSES = ((0,), (1, 2), (1, 2), (3,))


def partner_2(value, axis, bit):
    mask = 2**bit
    pairs = [(source, source ^ mask) for source in range(lax.axis_size(axis))]
    return lax.ppermute(value, axis, pairs)


def from_behind(block, axis, distance):
    devices = range(lax.axis_size(axis))
    route = [(i - distance, i) for i in devices if i - distance in devices]
    return lax.ppermute(block, axis, route)


def combine_pairs(products, weights):
    channels = products.shape[1]
    paired_shape = products.shape[:1] + (channels // 2, 2) + products.shape[2:]
    partner = jnp.flip(products.reshape(paired_shape), 2).reshape(products.shape)
    term_list = []
    for target in range(PHYS):
        running = jnp.zeros(products.shape[:2] + products.shape[3:], jnp.float32)
        for source in CLASSES[target]:
            running = running + weights[:, 0, source, target][None, :, None, None] * products[
                :, :, source
            ].astype(jnp.float32)
            running = running + weights[:, 1, source, target][None, :, None, None] * partner[
                :, :, source
            ].astype(jnp.float32)
        term_list.append(running.astype(jnp.bfloat16))
    return jnp.stack(term_list, axis=2)


def tile_contract(operands, weights, size, row_limit):
    rows_part, tensor, nearby = operands
    sectors_here = tensor.shape[0]
    padded = tensor.shape[1]
    full_rows = rows_part.shape[1]
    rows_cut = rows_part[:, :row_limit, :, :size]
    tensor_cut = tensor[:, :size, :, :size]
    near_cut = nearby[:, :, :size, :size]
    product_list = []
    for phys_state in range(PHYS):
        shifted = near_cut[CHARGE[phys_state] : CHARGE[phys_state] + sectors_here]
        product = jnp.einsum(
            "ixz,iczy->icxy",
            rows_cut[:, :, phys_state, :],
            shifted,
            preferred_element_type=jnp.float32,
        )
        product_list.append(product.astype(jnp.bfloat16))
    mixed_blocks = combine_pairs(jnp.stack(product_list, axis=2), weights)
    new_env = jnp.einsum(
        "icpxz,iypz->icxy", mixed_blocks, tensor_cut, preferred_element_type=jnp.float32
    ).astype(jnp.bfloat16)
    new_env = jnp.pad(new_env, ((0, 0), (0, 0), (0, full_rows - row_limit), (0, padded - size)))
    mixed_blocks = jnp.pad(
        mixed_blocks, ((0, 0), (0, 0), (0, 0), (0, full_rows - row_limit), (0, padded - size))
    )
    return (new_env, mixed_blocks)


def tile_gradient(operands, size):
    left_blocks, mixed_blocks = operands
    padded = left_blocks.shape[2]
    grad_part = jnp.einsum(
        "icxy,icpxz->iypz",
        left_blocks[:, :, :size, :],
        mixed_blocks[:, :, :, :size, :size],
        preferred_element_type=jnp.float32,
    )
    return jnp.pad(grad_part, ((0, 0), (0, 0), (0, 0), (0, padded - size)))


def local(site_tensor, left_env, boundary_env, sector_sizes, mpo_ops, mpo_mask):
    blocks = lax.axis_size("blk")
    sections = lax.axis_size("sect")
    per_sector = max(1, blocks // S)
    sectors_here = max(1, S // blocks)
    channels = W // per_sector
    padded = boundary_env.shape[1]
    position = lax.axis_index("blk")
    within = position % per_sector
    first_sector = position // per_sector * sectors_here
    first_channel = within * channels
    levels = per_sector.bit_length() - 1
    reach_count = (2 + sectors_here - 1) // sectors_here
    sizes_ext = jnp.concatenate([sector_sizes, jnp.zeros((2,), jnp.int32)])
    cell_index = jnp.arange(padded, dtype=jnp.int32)
    local_sizes = lax.dynamic_slice_in_dim(sizes_ext, first_sector, sectors_here + 2)
    small_only = jnp.all(local_sizes <= TILE)
    live_rows = (cell_index[None, :] < local_sizes[:, None]).astype(jnp.bfloat16)
    column_live = jnp.stack(
        [live_rows[CHARGE[p] : CHARGE[p] + sectors_here] for p in range(PHYS)], axis=1
    )
    tensor_mask = live_rows[:sectors_here, :, None, None] * column_live[:, None, :, :]
    column_mask = column_live[:, None, :, :]
    env_mask = live_rows[:sectors_here, None, :, None] * live_rows[:sectors_here, None, None, :]
    weights = lax.dynamic_slice_in_dim(
        mpo_ops * mpo_mask.astype(jnp.float32)[:, :, None, None], first_channel, channels, 0
    )
    left_blocks = left_env[0].reshape(sectors_here, channels, padded, padded)
    bound_blocks = boundary_env.reshape(sectors_here, channels, padded, padded) * env_mask

    def extend(current):
        pieces = [current]
        for offset_step in range(1, reach_count + 1):
            pieces.append(from_behind(current, "blk", -offset_step * per_sector))
        return jnp.concatenate(pieces, axis=0)

    def contract(rows_part, tensor, nearby):
        full_rows = rows_part.shape[1]
        small_rows = TILE
        small_path = partial(tile_contract, weights=weights, size=TILE, row_limit=small_rows)
        dense_path = partial(tile_contract, weights=weights, size=padded, row_limit=full_rows)
        return lax.cond(small_only, small_path, dense_path, (rows_part, tensor, nearby))

    def gradient_of(mixed_blocks):
        grad_part = lax.cond(
            small_only,
            partial(tile_gradient, size=TILE),
            partial(tile_gradient, size=padded),
            (left_blocks, mixed_blocks),
        )
        return grad_part * column_mask.astype(jnp.float32)

    section = lax.axis_index("sect")
    my_env = jnp.zeros_like(bound_blocks)
    pieces = site_tensor
    for sector_bit_number in range(levels):
        partner = partner_2(pieces, "blk", sector_bit_number)
        sector_upper_half = within >> sector_bit_number & 1
        pieces = jnp.where(
            sector_upper_half == 1,
            jnp.concatenate([partner, pieces], axis=1),
            jnp.concatenate([pieces, partner], axis=1),
        )
    tensor = pieces.reshape(sectors_here, padded, PHYS, padded) * tensor_mask
    current = extend(bound_blocks)
    held_state = jnp.zeros((sectors_here, padded, PHYS, padded), jnp.float32)
    for segment_index in range(sections):
        active = sections - 1 - segment_index
        if segment_index > 0:
            arrived = from_behind(my_env, "sect", -1)
            current = extend(arrived)

        def run_site(operands):
            new_env, mixed_blocks = contract(tensor, tensor, operands[0])
            return (new_env, gradient_of(mixed_blocks))

        def keep_state(operands):
            return (operands[1], operands[2])

        my_env, held_state = lax.cond(
            section == active, run_site, keep_state, (current, my_env, held_state)
        )
    grad_flat = held_state.reshape(sectors_here * padded, PHYS * padded)
    for bit_number in reversed(range(levels)):
        half_rows = grad_flat.shape[0] // 2
        upper_half = within >> bit_number & 1
        lower_part = grad_flat[:half_rows]
        upper_part = grad_flat[half_rows:]
        keep_part = jnp.where(upper_half == 1, upper_part, lower_part)
        send_part = jnp.where(upper_half == 1, lower_part, upper_part)
        grad_flat = keep_part + partner_2(send_part.astype(jnp.bfloat16), "blk", bit_number).astype(
            send_part.dtype
        )
    env_out = my_env.reshape(1, sectors_here * channels, padded, padded)
    return (env_out, grad_flat.astype(jnp.bfloat16)[None])


def solution(mesh):
    return jax.shard_map(
        local,
        mesh=mesh,
        in_specs=(
            P("sect", "blk", None),
            P("sect", "blk", None, None),
            P("blk", None, None),
            P(),
            P(),
            P(),
        ),
        out_specs=(P("sect", "blk", None, None), P("sect", "blk", None)),
        check_vma=False,
    )
```

profile of v0, /device:TPU:1, one launch (start us, length us, event | category | flops | bytes accessed | tf_op | source)
XLA Modules:
  0.0 600.4 jit_solution(7219138333437031436)
XLA Ops:
  7.0 8.7 %collective-permute-start = (bf16[1,48,1536]{2,1,0:T(8,128)(2,1)S(1)}, bf16[1,48,1536]{2,1,0:T(8,128)(2,1)S(1)}, u32[]{:S(2)}, u32[]{:S(2)}) collective-permute-start(bf16[1,48,1536]{2,1,0:T(8,128)(2,1)S(1)} %copy-done.15), channel_id=1, source_target_pairs={{0,1},{1,0},{2,3},{3,2},{4,5},{5,4},{6,7},{7,6},{8,9},{9,8},{10,11... | collective-permute-start | bytes 442376 | tf_op jit(solution)/shard_map/ppermute | solution.py:21
  17.1 1.9 collective-permute-start.1
  19.1 9.3 %collective-permute-done.1 = bf16[1,96,1536]{2,1,0:T(8,128)(2,1)S(1)} collective-permute-done((bf16[1,96,1536]{2,1,0:T(8,128)(2,1)S(1)}, bf16[1,96,1536]{2,1,0:T(8,128)(2,1)S(1)}, u32[]{:S(2)}, u32[]{:S(2)}) %collective-permute-start.1) | collective-permute-done | bytes 294944 | tf_op jit(solution)/shard_map/ppermute | solution.py:21
  28.5 4.1 collective-permute-start.2
  33.8 33.0 %collective-permute-done.3 = bf16[1,2,384,384]{2,3,1,0:T(8,128)(2,1)S(1)} collective-permute-done((bf16[1,2,384,384]{2,3,1,0:T(8,128)(2,1)S(1)}, bf16[1,2,384,384]{2,3,1,0:T(8,128)(2,1)S(1)}, u32[]{:S(2)}, u32[]{:S(2)}) %collective-permute-start.3) | collective-permute-done | bytes 589856 | tf_op jit(solution)/shard_map/ppermute | solution.py:27
  68.2 13.9 %collective-permute-done.2 = bf16[1,192,1536]{2,1,0:T(8,128)(2,1)} collective-permute-done((bf16[1,192,1536]{2,1,0:T(8,128)(2,1)S(1)}, bf16[1,192,1536]{2,1,0:T(8,128)(2,1)}, u32[]{:S(2)}, u32[]{:S(2)}) %collective-permute-start.2) | collective-permute-done | bytes 589856 | tf_op jit(solution)/shard_map/ppermute | solution.py:21
  82.1 2.3 concatenate.169
  84.4 4.9 fusion.340
  90.9 2.1 copy.53
  94.3 14.8 %collective-permute-done.5 = bf16[1,2,384,384]{2,3,1,0:T(8,128)(2,1)} collective-permute-done((bf16[1,2,384,384]{2,3,1,0:T(8,128)(2,1)}, bf16[1,2,384,384]{2,3,1,0:T(8,128)(2,1)}, u32[]{:S(2)}, u32[]{:S(2)}) %collective-permute-start.5) | collective-permute-done | bytes 589856 | tf_op jit(solution)/shard_map/ppermute | solution.py:27
  111.7 106.8 %collective-permute-done.6 = bf16[1,2,384,384]{2,3,1,0:T(8,128)(2,1)} collective-permute-done((bf16[1,2,384,384]{2,3,1,0:T(8,128)(2,1)}, bf16[1,2,384,384]{2,3,1,0:T(8,128)(2,1)}, u32[]{:S(2)}, u32[]{:S(2)}) %collective-permute-start.6) | collective-permute-done | bytes 589856 | tf_op jit(solution)/shard_map/ppermute | solution.py:27
  218.5 2.9 pad_maximum_fusion.13
  221.3 2.1 copy.56
  224.8 15.3 %collective-permute-done.8 = bf16[1,2,384,384]{2,3,1,0:T(8,128)(2,1)} collective-permute-done((bf16[1,2,384,384]{2,3,1,0:T(8,128)(2,1)}, bf16[1,2,384,384]{2,3,1,0:T(8,128)(2,1)}, u32[]{:S(2)}, u32[]{:S(2)}) %collective-permute-start.8) | collective-permute-done | bytes 589856 | tf_op jit(solution)/shard_map/ppermute | solution.py:27
  242.7 58.9 %collective-permute-done.10 = bf16[1,2,384,384]{2,3,1,0:T(8,128)(2,1)} collective-permute-done((bf16[1,2,384,384]{2,3,1,0:T(8,128)(2,1)}, bf16[1,2,384,384]{2,3,1,0:T(8,128)(2,1)}, u32[]{:S(2)}, u32[]{:S(2)}) %collective-permute-start.10) | collective-permute-done | bytes 589856 | tf_op jit(solution)/shard_map/ppermute | solution.py:27
  301.5 59.9 %collective-permute-done.9 = bf16[1,2,384,384]{2,3,1,0:T(8,128)(2,1)} collective-permute-done((bf16[1,2,384,384]{2,3,1,0:T(8,128)(2,1)}, bf16[1,2,384,384]{2,3,1,0:T(8,128)(2,1)}, u32[]{:S(2)}, u32[]{:S(2)}) %collective-permute-start.9) | collective-permute-done | bytes 589856 | tf_op jit(solution)/shard_map/ppermute | solution.py:27
  361.4 2.9 pad_maximum_fusion.14
  364.3 7.7 %conditional.14 = ((bf16[1,2,384,384]{3,2,1,0:T(8,128)(2,1)}, f32[1,384,4,384]{3,1,2,0:T(8,128)S(1)})) conditional(s32[]{:T(128)} %convert_element_type.818, (bf16[1,2,384,384]{3,2,1,0:T(8,128)(2,1)}, f32[1,384,4,384]{3,1,2,0:T(8,128)S(1)}) %get-tuple-element.647, (pred[]{:T(512)}, f32[2,2,4,4]{0,3,2,1:T(4,128)S(1)}, ...), branch_computations={%region_13.14_spmd, %region_14.19_spmd} | conditional | flops 2732951040 | bytes 46284256 | solution.py:168
  372.0 2.1 copy.59
  375.4 15.3 %collective-permute-done.11 = bf16[1,2,384,384]{2,3,1,0:T(8,128)(2,1)} collective-permute-done((bf16[1,2,384,384]{2,3,1,0:T(8,128)(2,1)}, bf16[1,2,384,384]{2,3,1,0:T(8,128)(2,1)}, u32[]{:S(2)}, u32[]{:S(2)}) %collective-permute-start.11) | collective-permute-done | bytes 589856 | tf_op jit(solution)/shard_map/ppermute | solution.py:27
  393.3 23.1 %collective-permute-done.12 = bf16[1,2,384,384]{2,3,1,0:T(8,128)(2,1)} collective-permute-done((bf16[1,2,384,384]{2,3,1,0:T(8,128)(2,1)}, bf16[1,2,384,384]{2,3,1,0:T(8,128)(2,1)}, u32[]{:S(2)}, u32[]{:S(2)}) %collective-permute-start.12) | collective-permute-done | bytes 589856 | tf_op jit(solution)/shard_map/ppermute | solution.py:27
  416.4 6.6 %collective-permute-done.13 = bf16[1,2,384,384]{2,3,1,0:T(8,128)(2,1)} collective-permute-done((bf16[1,2,384,384]{2,3,1,0:T(8,128)(2,1)}, bf16[1,2,384,384]{2,3,1,0:T(8,128)(2,1)}, u32[]{:S(2)}, u32[]{:S(2)}) %collective-permute-start.13) | collective-permute-done | bytes 589856 | tf_op jit(solution)/shard_map/ppermute | solution.py:27
  423.1 2.9 pad_maximum_fusion.15
  425.9 15.4 %conditional.15 = ((bf16[1,2,384,384]{3,2,1,0:T(8,128)(2,1)}, f32[1,384,4,384]{3,1,2,0:T(8,128)S(1)})) conditional(s32[]{:T(128)} %convert_element_type.817, (bf16[1,2,384,384]{3,2,1,0:T(8,128)(2,1)}, f32[1,384,4,384]{3,1,2,0:T(8,128)S(1)}) %get-tuple-element.648, (pred[]{:T(512)}, f32[2,2,4,4]{0,3,2,1:T(4,128)S(1)}, ...), branch_computations={%region_19.20_spmd.clone, %region_20.25_spmd.clone} | conditional | flops 2732951040 | bytes 48655896 | solution.py:168
  426.8 7.0 %conditional.16 = (bf16[1,2,384,384]{3,2,1,0:T(8,128)(2,1)}, bf16[1,2,4,384,384]{3,4,1,2,0:T(8,128)(2,1)S(1)}) conditional(s32[]{:T(128)} %convert_element_type.831, (f32[2,2,4,4]{0,3,2,1:T(4,128)S(1)}, bf16[1,2,384,384]{2,3,1,0:T(8,128)(2,1)}, bf16[1,384,4,384]{3,1,2,0:T(8,128)(2,1)S(1)}, bf16[1,2,384,384]{2,3,1,0:T(8,128)(2,1)}, ...), branch_computations={%region_21.21_spmd, %region_22.22_spmd} | conditional | flops 1826390016 | bytes 28901736 | solution.py:130
  434.1 5.4 conditional.17
  434.2 2.6 copy.49
  442.1 23.2 %collective-permute-start.14 = (bf16[192,1536]{1,0:T(8,128)(2,1)S(1)}, bf16[192,1536]{1,0:T(8,128)(2,1)S(1)}, u32[]{:S(2)}, u32[]{:S(2)}) collective-permute-start(bf16[192,1536]{1,0:T(8,128)(2,1)S(1)} %bitcast.935), channel_id=1, source_target_pairs={{0,4},{1,5},{2,6},{3,7},{4,0},{5,1},{6,2},{7,3},{8,12},{9,13},{10,... | collective-permute-start | bytes 1769480 | tf_op jit(solution)/shard_map/ppermute | solution.py:21
  466.3 15.2 %collective-permute-done.14 = bf16[192,1536]{1,0:T(8,128)(2,1)S(1)} collective-permute-done((bf16[192,1536]{1,0:T(8,128)(2,1)S(1)}, bf16[192,1536]{1,0:T(8,128)(2,1)S(1)}, u32[]{:S(2)}, u32[]{:S(2)}) %collective-permute-start.14) | collective-permute-done | bytes 589856 | tf_op jit(solution)/shard_map/ppermute | solution.py:21
  481.7 106.8 %collective-permute-start.15 = (bf16[96,1536]{1,0:T(8,128)(2,1)S(1)}, bf16[96,1536]{1,0:T(8,128)(2,1)S(1)}, u32[]{:S(2)}, u32[]{:S(2)}) collective-permute-start(bf16[96,1536]{1,0:T(8,128)(2,1)S(1)} %select_convert_fusion.1), channel_id=1, source_target_pairs={{0,2},{1,3},{2,0},{3,1},{4,6},{5,7},{6,4},{7,5},{8,10},{9,11},{10,... | collective-permute-start | bytes 884744 | tf_op jit(solution)/shard_map/ppermute | solution.py:21
  588.5 5.9 collective-permute-done.15
  594.5 4.0 collective-permute-start.16
  (81 shorter events, 40.0 us)
Async XLA Ops:
  2.2 0.5 copy-start.17
  2.9 4.1 copy-start.15
  4.3 12.1 %copy-start.19 = (s32[16,2]{0,1:T(2,128)S(1)}, s32[16,2]{0,1:T(2,128)}, u32[]{:S(2)}) copy-start(s32[16,2]{0,1:T(2,128)} %param.35) | copy-start | bytes 388
  4.4 62.4 %collective-permute-start.3 = (bf16[1,2,384,384]{2,3,1,0:T(8,128)(2,1)S(1)}, bf16[1,2,384,384]{2,3,1,0:T(8,128)(2,1)S(1)}, u32[]{:S(2)}, u32[]{:S(2)}) collective-permute-start(bf16[1,2,384,384]{2,3,1,0:T(8,128)(2,1)S(1)} %multiply_bitcast_fusion), channel_id=1, source_target_pairs={{8,0},{9,1},{10,2},{11,3},{12,4},{13,5},{14,6},{15,7},{16,8},{17,9... | collective-permute-start | bytes 1769480 | tf_op jit(solution)/shard_map/ppermute | solution.py:27
  5.7 61.1 %collective-permute-start.4 = (bf16[1,2,384,384]{2,3,1,0:T(8,128)(2,1)S(1)}, bf16[1,2,384,384]{2,3,1,0:T(8,128)(2,1)S(1)}, u32[]{:S(2)}, u32[]{:S(2)}) collective-permute-start(bf16[1,2,384,384]{2,3,1,0:T(8,128)(2,1)S(1)} %multiply_bitcast_fusion), channel_id=1, source_target_pairs={{16,0},{17,1},{18,2},{19,3},{20,4},{21,5},{22,6},{23,7},{24,8},{25... | collective-permute-start | bytes 1769480 | tf_op jit(solution)/shard_map/ppermute | solution.py:27
  7.0 10.0 %collective-permute-start = (bf16[1,48,1536]{2,1,0:T(8,128)(2,1)S(1)}, bf16[1,48,1536]{2,1,0:T(8,128)(2,1)S(1)}, u32[]{:S(2)}, u32[]{:S(2)}) collective-permute-start(bf16[1,48,1536]{2,1,0:T(8,128)(2,1)S(1)} %copy-done.15), channel_id=1, source_target_pairs={{0,1},{1,0},{2,3},{3,2},{4,5},{5,4},{6,7},{7,6},{8,9},{9,8},{10,11... | collective-permute-start | bytes 442376 | tf_op jit(solution)/shard_map/ppermute | solution.py:21
  17.0 15.6 %copy-start.18 = (f32[16,2,4,4]{0,3,2,1:T(4,128)S(1)}, f32[16,2,4,4]{0,3,2,1:T(4,128)}, u32[]{:S(2)}) copy-start(f32[16,2,4,4]{0,3,2,1:T(4,128)} %param.34) | copy-start | bytes 6148
  17.1 11.3 %collective-permute-start.1 = (bf16[1,96,1536]{2,1,0:T(8,128)(2,1)S(1)}, bf16[1,96,1536]{2,1,0:T(8,128)(2,1)S(1)}, u32[]{:S(2)}, u32[]{:S(2)}) collective-permute-start(bf16[1,96,1536]{2,1,0:T(8,128)(2,1)S(1)} %maximum_select_fusion.3), channel_id=1, source_target_pairs={{0,2},{1,3},{2,0},{3,1},{4,6},{5,7},{6,4},{7,5},{8,10},{9,11},{10,... | collective-permute-start | bytes 884744 | tf_op jit(solution)/shard_map/ppermute | solution.py:21
  28.5 53.6 %collective-permute-start.2 = (bf16[1,192,1536]{2,1,0:T(8,128)(2,1)S(1)}, bf16[1,192,1536]{2,1,0:T(8,128)(2,1)}, u32[]{:S(2)}, u32[]{:S(2)}) collective-permute-start(bf16[1,192,1536]{2,1,0:T(8,128)(2,1)S(1)} %maximum_select_fusion.1), channel_id=1, source_target_pairs={{0,4},{1,5},{2,6},{3,7},{4,0},{5,1},{6,2},{7,3},{8,12},{9,13},{10,... | collective-permute-start | bytes 1769480 | tf_op jit(solution)/shard_map/ppermute | solution.py:21
  93.0 16.1 %collective-permute-start.5 = (bf16[1,2,384,384]{2,3,1,0:T(8,128)(2,1)}, bf16[1,2,384,384]{2,3,1,0:T(8,128)(2,1)}, u32[]{:S(2)}, u32[]{:S(2)}) collective-permute-start(bf16[1,2,384,384]{2,3,1,0:T(8,128)(2,1)} %copy.53), channel_id=1, source_target_pairs={{128,0},{256,128},{384,256},{129,1},{257,129},{385,257},{130,2},{2... | collective-permute-start | bytes 1769480 | tf_op jit(solution)/shard_map/ppermute | solution.py:27
  109.1 109.4 %collective-permute-start.6 = (bf16[1,2,384,384]{2,3,1,0:T(8,128)(2,1)}, bf16[1,2,384,384]{2,3,1,0:T(8,128)(2,1)}, u32[]{:S(2)}, u32[]{:S(2)}) collective-permute-start(bf16[1,2,384,384]{2,3,1,0:T(8,128)(2,1)} %collective-permute-done.5), channel_id=1, source_target_pairs={{8,0},{9,1},{10,2},{11,3},{12,4},{13,5},{14,6},{15,7},{16,8},{17,9... | collective-permute-start | bytes 1769480 | tf_op jit(solution)/shard_map/ppermute | solution.py:27
  110.4 108.1 %collective-permute-start.7 = (bf16[1,2,384,384]{2,3,1,0:T(8,128)(2,1)}, bf16[1,2,384,384]{2,3,1,0:T(8,128)(2,1)}, u32[]{:S(2)}, u32[]{:S(2)}) collective-permute-start(bf16[1,2,384,384]{2,3,1,0:T(8,128)(2,1)} %collective-permute-done.5), channel_id=1, source_target_pairs={{16,0},{17,1},{18,2},{19,3},{20,4},{21,5},{22,6},{23,7},{24,8},{25... | collective-permute-start | bytes 1769480 | tf_op jit(solution)/shard_map/ppermute | solution.py:27
  223.5 16.6 %collective-permute-start.8 = (bf16[1,2,384,384]{2,3,1,0:T(8,128)(2,1)}, bf16[1,2,384,384]{2,3,1,0:T(8,128)(2,1)}, u32[]{:S(2)}, u32[]{:S(2)}) collective-permute-start(bf16[1,2,384,384]{2,3,1,0:T(8,128)(2,1)} %copy.56), channel_id=1, source_target_pairs={{128,0},{256,128},{384,256},{129,1},{257,129},{385,257},{130,2},{2... | collective-permute-start | bytes 1769480 | tf_op jit(solution)/shard_map/ppermute | solution.py:27
  240.1 61.5 %collective-permute-start.10 = (bf16[1,2,384,384]{2,3,1,0:T(8,128)(2,1)}, bf16[1,2,384,384]{2,3,1,0:T(8,128)(2,1)}, u32[]{:S(2)}, u32[]{:S(2)}) collective-permute-start(bf16[1,2,384,384]{2,3,1,0:T(8,128)(2,1)} %collective-permute-done.8), channel_id=1, source_target_pairs={{16,0},{17,1},{18,2},{19,3},{20,4},{21,5},{22,6},{23,7},{24,8},{25... | collective-permute-start | bytes 1769480 | tf_op jit(solution)/shard_map/ppermute | solution.py:27
  241.4 120.1 %collective-permute-start.9 = (bf16[1,2,384,384]{2,3,1,0:T(8,128)(2,1)}, bf16[1,2,384,384]{2,3,1,0:T(8,128)(2,1)}, u32[]{:S(2)}, u32[]{:S(2)}) collective-permute-start(bf16[1,2,384,384]{2,3,1,0:T(8,128)(2,1)} %collective-permute-done.8), channel_id=1, source_target_pairs={{8,0},{9,1},{10,2},{11,3},{12,4},{13,5},{14,6},{15,7},{16,8},{17,9... | collective-permute-start | bytes 1769480 | tf_op jit(solution)/shard_map/ppermute | solution.py:27
  374.1 16.6 %collective-permute-start.11 = (bf16[1,2,384,384]{2,3,1,0:T(8,128)(2,1)}, bf16[1,2,384,384]{2,3,1,0:T(8,128)(2,1)}, u32[]{:S(2)}, u32[]{:S(2)}) collective-permute-start(bf16[1,2,384,384]{2,3,1,0:T(8,128)(2,1)} %copy.59), channel_id=1, source_target_pairs={{128,0},{256,128},{384,256},{129,1},{257,129},{385,257},{130,2},{2... | collective-permute-start | bytes 1769480 | tf_op jit(solution)/shard_map/ppermute | solution.py:27
  390.7 25.7 %collective-permute-start.12 = (bf16[1,2,384,384]{2,3,1,0:T(8,128)(2,1)}, bf16[1,2,384,384]{2,3,1,0:T(8,128)(2,1)}, u32[]{:S(2)}, u32[]{:S(2)}) collective-permute-start(bf16[1,2,384,384]{2,3,1,0:T(8,128)(2,1)} %collective-permute-done.11), channel_id=1, source_target_pairs={{8,0},{9,1},{10,2},{11,3},{12,4},{13,5},{14,6},{15,7},{16,8},{17,9... | collective-permute-start | bytes 1769480 | tf_op jit(solution)/shard_map/ppermute | solution.py:27
  392.0 31.1 %collective-permute-start.13 = (bf16[1,2,384,384]{2,3,1,0:T(8,128)(2,1)}, bf16[1,2,384,384]{2,3,1,0:T(8,128)(2,1)}, u32[]{:S(2)}, u32[]{:S(2)}) collective-permute-start(bf16[1,2,384,384]{2,3,1,0:T(8,128)(2,1)} %collective-permute-done.11), channel_id=1, source_target_pairs={{16,0},{17,1},{18,2},{19,3},{20,4},{21,5},{22,6},{23,7},{24,8},{25... | collective-permute-start | bytes 1769480 | tf_op jit(solution)/shard_map/ppermute | solution.py:27
  426.8 7.0 %copy-start = (bf16[1,2,384,384]{3,2,1,0:T(8,128)(2,1)S(1)}, bf16[1,2,384,384]{3,2,1,0:T(8,128)(2,1)}, u32[]{:S(2)}) copy-start(bf16[1,2,384,384]{3,2,1,0:T(8,128)(2,1)} %get-tuple-element.474) | copy-start | bytes 1769476 | tf_op jit(solution)/shard_map/cond
  426.8 4.6 copy-start.9
  434.1 5.4 copy-start.16
  442.1 39.4 %collective-permute-start.14 = (bf16[192,1536]{1,0:T(8,128)(2,1)S(1)}, bf16[192,1536]{1,0:T(8,128)(2,1)S(1)}, u32[]{:S(2)}, u32[]{:S(2)}) collective-permute-start(bf16[192,1536]{1,0:T(8,128)(2,1)S(1)} %bitcast.935), channel_id=1, source_target_pairs={{0,4},{1,5},{2,6},{3,7},{4,0},{5,1},{6,2},{7,3},{8,12},{9,13},{10,... | collective-permute-start | bytes 1769480 | tf_op jit(solution)/shard_map/ppermute | solution.py:21
  481.7 112.6 %collective-permute-start.15 = (bf16[96,1536]{1,0:T(8,128)(2,1)S(1)}, bf16[96,1536]{1,0:T(8,128)(2,1)S(1)}, u32[]{:S(2)}, u32[]{:S(2)}) collective-permute-start(bf16[96,1536]{1,0:T(8,128)(2,1)S(1)} %select_convert_fusion.1), channel_id=1, source_target_pairs={{0,2},{1,3},{2,0},{3,1},{4,6},{5,7},{6,4},{7,5},{8,10},{9,11},{10,... | collective-permute-start | bytes 884744 | tf_op jit(solution)/shard_map/ppermute | solution.py:21
  594.5 5.0 collective-permute-start.16
where the time goes:
time: 612 us; the launch traced here: 600 us
  waiting for transfers between devices  379 us (62%)
  starting transfers between devices  163 us (27%)
  other arithmetic  22.5 us (4%)
  local copies, waits for them, and re-layouts  19.1 us (3%)
  loops' own time  9.01 us (1%)
  matrix products  6.66 us (1%)
    ppermute x11, waiting for transfers between devices, from_behind(): return lax.ppermute(block, axis, route)  334 us
    ppermute x6, starting transfers between devices, partner_2(): return lax.ppermute(value, axis, pairs)  149 us
    ppermute x6, waiting for transfers between devices, partner_2(): return lax.ppermute(value, axis, pairs)  45.3 us
    ppermute x11, starting transfers between devices, from_behind(): return lax.ppermute(block, axis, route)  14.1 us
  transfers between devices with their start and end apart: 17, of which 14 were waited for; matrix products, arithmetic and copies ran while one was open for 1% of the time, Pallas kernels for 0%

commit v1 on v0

v1 whole, which is shorter than its diff:
```python
from functools import partial

import jax
import jax.numpy as jnp
from jax import lax
from jax.experimental import pallas as pl
from jax.experimental.pallas import tpu as pltpu
from jax.sharding import PartitionSpec as P

S = 16
W = 16
N = 384
T = 128
H = 112
G8 = 8
BF = jnp.bfloat16
F32 = jnp.float32


def mm(a, b):
    return jnp.dot(a, b, preferred_element_type=F32)


def mm_t(a, b):
    return lax.dot_general(a, b, (((1,), (1,)), ((), ())), preferred_element_type=F32)


def t_mm(a, b):
    return lax.dot_general(a, b, (((0,), (0,)), ((), ())), preferred_element_type=F32)


def mix(wts, prods, target):
    sources = ((0,), (1, 2), (1, 2), (3,))[target]
    out = []
    for w in range(2):
        total = None
        for p in sources:
            for k in range(2):
                coef = wts[((w * 2 + k) * 4 + p) * 4 + target]
                term = coef * prods[w ^ k][p].astype(F32)
                total = term if total is None else total + term
        out.append(total.astype(BF))
    return out


def push_mixed(wts, acol, r_ref, size):
    prods = []
    for w in range(2):
        right = r_ref[w, :size, :size]
        own = mm(acol[:size, :size], right).astype(BF)
        halo = mm(acol[N : 2 * N, :size], right).astype(BF)
        prods.append((own, halo[:T], halo[T : 2 * T], halo[2 * T :]))
    return [mix(wts, prods, target) for target in range(4)]


def pull_mixed(wts, pull, base, m1, m3):
    prods = []
    zero = jnp.zeros((T - H, T), BF)
    for w in range(2):
        near = jnp.concatenate([m1[w], zero], axis=0)
        far = jnp.concatenate([m3[w], zero], axis=0)
        prods.append(
            (
                None,
                mm(pull[:, base : base + T], near).astype(BF),
                mm(pull[:, base + T : base + 2 * T], near).astype(BF),
                mm(pull[:, base + 2 * T : base + 3 * T], far).astype(BF),
            )
        )
    return [None] + [mix(wts, prods, target) for target in range(1, 4)]


def push_send(info, wts, acol, r_ref, c0_out, m1_out, m3_out):
    def run(size):
        mixed = push_mixed(wts, acol, r_ref, size)
        for w in range(2):
            c0_out[w, :size, :size] = mm_t(mixed[0][w], acol[:size, :size]).astype(BF)
            near = mm_t(mixed[1][w], acol[N : N + T, :size]) + mm_t(
                mixed[2][w], acol[N + T : N + 2 * T, :size]
            )
            far = mm_t(mixed[3][w], acol[N + 2 * T : 2 * N, :size])
            tile = r_ref[w, :H, :T]
            m1_out[w] = jnp.where(info[1] == 1, tile, near[:H].astype(BF))
            m3_out[w] = jnp.where(info[2] == 1, tile, far[:H].astype(BF))

    @pl.when(info[0] == 1)
    def _():
        run(N)

    @pl.when(info[0] == 0)
    def _():
        run(T)


def combine(info, wts, pull, base, c0, m1, m3, r_out):
    @pl.when(info[0] == 1)
    def _():
        mixed = pull_mixed(wts, pull, base, m1, m3)
        for w in range(2):
            total = c0[w].astype(F32)
            for p in range(1, 4):
                total = total + mm_t(mixed[p][w], pull[:, base + (p - 1) * T : base + p * T])
            r_out[w] = total.astype(BF)

    @pl.when(info[0] == 0)
    def _():
        r_out[...] = jnp.zeros_like(r_out)
        for w in range(2):
            r_out[w, :H, :T] = (
                c0[w, :H, :T].astype(F32) + m1[w].astype(F32) + m3[w].astype(F32)
            ).astype(BF)


def first_kernel(info, wts, ag, bound, acol, pull, r_out, c0_out, m1_out, m3_out):
    for within in range(G8):
        core, pos = within % 2, within // 2
        rows = lax.broadcasted_iota(jnp.int32, (48, 3 * N), 0) + 48 * within
        own = jnp.where(rows < info[3], ag[core, pos, :48, :], jnp.zeros((48, 3 * N), BF))
        acol[48 * within : 48 * within + 48, :] = own[:, :N]
        pull[48 * within : 48 * within + 48, :] = own[:, N:]
        halo_rows = lax.broadcasted_iota(jnp.int32, (16, N), 0) + 16 * within
        for block in range(3):
            limit = info[4] if block < 2 else info[5]
            at = N + T * block + 16 * within
            acol[at : at + 16, :] = jnp.where(
                halo_rows < limit,
                ag[core, pos, 48:, N * block : N * block + N],
                jnp.zeros((16, N), BF),
            )
    row = lax.broadcasted_iota(jnp.int32, (N, N), 0)
    col = lax.broadcasted_iota(jnp.int32, (N, N), 1)
    live = jnp.maximum(row, col) < info[3]
    for w in range(2):
        r_out[w] = jnp.where(live, bound[w], jnp.zeros((N, N), BF))

    @pl.when(info[6] == 3)
    def _():
        push_send(info, wts, acol, r_out, c0_out, m1_out, m3_out)


def next_kernel(active, info, wts, acol, pull, c0, m1, m3, r_in, s1_in, s3_in, r_out, s1, s3, c0_out, m1_out, m3_out):
    del r_in, s1_in, s3_in

    @pl.when(info[6] == active)
    def _():
        combine(info, wts, pull, N, c0, m1, m3, r_out)
        s1[...] = m1[...]
        s3[...] = m3[...]
        push_send(info, wts, acol, r_out, c0_out, m1_out, m3_out)


def last_kernel(info, wts, pull, c0, m1, m3, r_out):
    combine(info, wts, pull, 0, c0, m1, m3, r_out)


def write_rows(out, grads, at, size):
    for within in range(G8):
        spot = (within % 2) * 4 + within // 2
        out[spot, :, at : at + size] = grads[48 * within : 48 * within + 48].astype(BF)


def push_grad_kernel(info, wts, acol, r_ref, left, near, far, out):
    def run(size):
        mixed = push_mixed(wts, acol, r_ref, size)
        if size < N:
            out[...] = jnp.zeros_like(out)
        own = t_mm(left[0, :size, :], mixed[0][0]) + t_mm(left[1, :size, :], mixed[0][1])
        write_rows(out, own, 0, size)
        for p in (1, 2):
            part = t_mm(near[0], mixed[p][0][:H]) + t_mm(near[1], mixed[p][1][:H])
            write_rows(out, part, N * p, size)
        part = t_mm(far[0], mixed[3][0][:H]) + t_mm(far[1], mixed[3][1][:H])
        write_rows(out, part, N * 3, size)

    @pl.when(info[0] == 1)
    def _():
        run(N)

    @pl.when(info[0] == 0)
    def _():
        run(T)


def pull_grad_kernel(info, wts, pull, left, m1, m3, out):
    @pl.when(info[0] == 1)
    def _():
        mixed = pull_mixed(wts, pull, 0, m1, m3)
        for p in range(1, 4):
            part = t_mm(left[0], mixed[p][0]) + t_mm(left[1], mixed[p][1])
            write_rows(out, part, T * (p - 1), T)

    @pl.when(info[0] == 0)
    def _():
        out[...] = jnp.zeros_like(out)


SMEM = pl.BlockSpec(memory_space=pltpu.SMEM)
VMEM = pl.BlockSpec(memory_space=pltpu.VMEM)
PARAMS = pltpu.CompilerParams(vmem_limit_bytes=48 * 1024 * 1024)
R_T = jax.ShapeDtypeStruct((2, N, N), BF)
M_T = jax.ShapeDtypeStruct((2, H, T), BF)


def call(kernel, outs, count, name, **extra):
    return pl.pallas_call(
        kernel,
        out_shape=outs,
        in_specs=[SMEM, SMEM] + [VMEM] * count,
        out_specs=jax.tree.map(lambda _: VMEM, outs),
        compiler_params=PARAMS,
        name=name,
        **extra,
    )


def local(site_tensor, left_env, boundary_env, sector_sizes, mpo_ops, mpo_mask):
    section = lax.axis_index("sect")
    position = lax.axis_index("blk")
    within = position % G8
    sector = position // G8
    blk_devices = 128

    sizes_pad = jnp.concatenate(
        [jnp.zeros((2,), jnp.int32), sector_sizes.astype(jnp.int32)]
    )
    near_sizes = lax.dynamic_slice_in_dim(sizes_pad, sector, 3)
    n_far, n_near, n_own = near_sizes[0], near_sizes[1], near_sizes[2]
    info = jnp.stack(
        [
            (n_own > H).astype(jnp.int32),
            (n_near > H).astype(jnp.int32),
            (n_far > H).astype(jnp.int32),
            n_own,
            n_near,
            n_far,
            section,
            sector,
        ]
    )
    wts = lax.dynamic_slice_in_dim(
        mpo_ops * mpo_mask.astype(F32)[:, :, None, None], within * 2, 2, 0
    ).reshape(64)

    def blk_perm(value, pairs):
        return lax.ppermute(value, "blk", pairs)

    def both_perm(value, pairs):
        return lax.ppermute(value, ("sect", "blk"), pairs)

    def partner(value, mask):
        return blk_perm(value, [(i, i ^ mask) for i in range(blk_devices)])

    rows = site_tensor[0]
    narrow = jnp.concatenate([rows[:, N * p : N * p + T] for p in range(1, 4)], axis=1)
    above = lax.ppermute(narrow, "sect", [(i + 1, i) for i in range(3)])
    halo = jnp.zeros((16, 3 * N), BF)
    pieces = []
    for j in range(3):
        near_pairs = [
            (q * 8 + a, (q + 1) * 8 + 3 * a + j)
            for q in range(S - 1)
            for a in range(3)
            if 3 * a + j < 8
        ]
        far_pairs = [
            (q * 8 + a, (q + 2) * 8 + 3 * a + j)
            for q in range(S - 2)
            for a in range(3)
            if 3 * a + j < 8
        ]
        cut = rows[16 * j : 16 * j + 16]
        pieces.append(
            jnp.concatenate(
                [blk_perm(cut[:, N : 3 * N], near_pairs), blk_perm(cut[:, 3 * N :], far_pairs)],
                axis=1,
            )
        )
    halo = jnp.where(within % 3 == 0, pieces[0], jnp.where(within % 3 == 1, pieces[1], pieces[2]))
    packed = jnp.concatenate(
        [jnp.concatenate([rows[:, :N], narrow, above], axis=1), halo], axis=0
    )[None]
    for mask in (2, 4):
        other = partner(packed, mask)
        packed = jnp.where(
            (within & mask) > 0,
            jnp.concatenate([other, packed], axis=0),
            jnp.concatenate([packed, other], axis=0),
        )
    other = partner(packed, 1)
    gathered = jnp.where(
        (within & 1) > 0, jnp.stack([other, packed]), jnp.stack([packed, other])
    )

    left = left_env[0]
    gathered, left_tile = lax.optimization_barrier((gathered, left[:, :H, :]))
    left_near = blk_perm(left_tile, [(i, i + 8) for i in range(blk_devices - 8)])
    left_far = blk_perm(left_tile, [(i, i + 16) for i in range(blk_devices - 16)])

    acol_t = jax.ShapeDtypeStruct((2 * N, N), BF)
    acol, pull, right, c0, m1, m3 = call(
        first_kernel, (acol_t, jax.ShapeDtypeStruct((N, 2 * N), BF), R_T, R_T, M_T, M_T), 2, "first"
    )(info, wts, gathered, boundary_env)
    seen1 = jnp.zeros((2, H, T), BF)
    seen3 = jnp.zeros((2, H, T), BF)

    def shift(value, site, step, target):
        return both_perm(
            value,
            [
                (site * blk_devices + i, target * blk_devices + i - step)
                for i in range(step, blk_devices)
            ],
        )

    for site in (3, 2, 1):
        got0 = shift(c0, site, 0, site - 1)
        got1 = shift(m1, site, 8, site - 1)
        got3 = shift(m3, site, 16, site - 1)
        right, seen1, seen3, c0, m1, m3 = call(
            partial(next_kernel, site - 1),
            (R_T, M_T, M_T, R_T, M_T, M_T),
            8,
            "next",
            input_output_aliases={7: 0, 8: 1, 9: 2},
        )(info, wts, acol, pull, got0, got1, got3, right, seen1, seen3)
    got1 = shift(m1, 0, 8, 0)
    got3 = shift(m3, 0, 16, 0)
    push_part = call(
        push_grad_kernel, jax.ShapeDtypeStruct((G8, 48, 4 * N), BF), 5, "push_grad"
    )(info, wts, acol, right, left, left_near, left_far)

    up = [(i, i + 1) for i in range(3)]
    back = lax.ppermute(right, "sect", up)
    back1 = lax.ppermute(seen1, "sect", up)
    back3 = lax.ppermute(seen3, "sect", up)
    final = call(last_kernel, R_T, 4, "last")(info, wts, pull, c0, got1, got3)
    env_out = jnp.where(section == 0, final, back)
    at1 = jnp.where(section == 0, got1, back1)
    at3 = jnp.where(section == 0, got3, back3)
    pull_part = call(pull_grad_kernel, jax.ShapeDtypeStruct((G8, 48, N), BF), 4, "pull_grad")(
        info, wts, pull, left, at1, at3
    )

    def scatter(part):
        for mask in (1, 4, 2):
            half = part.shape[0] // 2
            upper = (within & mask) > 0
            send = jnp.where(upper, part[:half], part[half:])
            keep = jnp.where(upper, part[half:], part[:half])
            part = (keep.astype(F32) + partner(send, mask).astype(F32)).astype(BF)
        return part[0]

    push_sum = scatter(push_part)
    pull_sum = scatter(pull_part)
    near_sum = blk_perm(push_sum[:, N : 3 * N], [(i, i - 8) for i in range(8, blk_devices)])
    far_sum = blk_perm(push_sum[:, 3 * N :], [(i, i - 16) for i in range(16, blk_devices)])
    wide = jnp.pad(pull_sum.reshape(48, 3, T), ((0, 0), (0, 0), (0, N - T))).reshape(48, 3 * N)
    rest = jnp.where(n_own > H, wide, jnp.concatenate([near_sum, far_sum], axis=1))
    grads = jnp.concatenate([push_sum[:, :N], rest], axis=1)
    return env_out[None].reshape(1, 2, N, N), grads[None]


def solution(mesh):
    return jax.shard_map(
        local,
        mesh=mesh,
        in_specs=(
            P("sect", "blk", None),
            P("sect", "blk", None, None),
            P("blk", None, None),
            P(),
            P(),
            P(),
        ),
        out_specs=(P("sect", "blk", None, None), P("sect", "blk", None)),
        check_vma=False,
    )
```

time: 612 us -> 240 us (0.39)
  the two profiles are of different devices: /device:TPU:1 before, /device:TPU:3 now
where the time goes in v1:
time: 240 us; the launch traced here: 239 us
  waiting for transfers between devices  124 us (52%)
  starting transfers between devices  95.5 us (40%)
  local copies, waits for them, and re-layouts  6.95 us (3%)
  Pallas kernels  6.08 us (3%)
  between operations  3.21 us (1%)
  other arithmetic  2.95 us (1%)
    ppermute x11, waiting for transfers between devices, both_perm(): return lax.ppermute(value, ('sect', 'blk'), pairs)  66.4 us
    ppermute x19, starting transfers between devices, blk_perm(): return lax.ppermute(value, 'blk', pairs)  64.4 us
    ppermute x19, waiting for transfers between devices, blk_perm(): return lax.ppermute(value, 'blk', pairs)  54.4 us
    ppermute x11, starting transfers between devices, both_perm(): return lax.ppermute(value, ('sect', 'blk'), pairs)  21.9 us
  transfers between devices with their start and end apart: 34, of which 11 were waited for; matrix products, arithmetic and copies ran while one was open for 3% of the time, Pallas kernels for 2%

profile of v1, /device:TPU:3, one launch (start us, length us, event | category | flops | bytes accessed | tf_op | source)
XLA Modules:
  0.0 238.9 jit_solution(12624057299011912456)
XLA Ops:
  1.5 15.0 %collective-permute-start.2 = (bf16[16,384]{1,0:T(8,128)(2,1)S(1)}, bf16[16,384]{1,0:T(8,128)(2,1)S(1)}, u32[]{:S(2)}, u32[]{:S(2)}) collective-permute-start(bf16[16,384]{1,0:T(8,128)(2,1)S(1)} %slice.158), channel_id=1, source_target_pairs={{0,16},{1,19},{2,22},{8,24},{9,27},{10,30},{16,32},{17,35},{18,38}... | collective-permute-start | bytes 36872 | tf_op jit(solution)/shard_map/ppermute | solution.py:245
  17.9 1.9 collective-permute-start.4
  19.8 1.9 collective-permute-start.3
  26.0 6.7 %collective-permute-done.4 = bf16[16,384]{1,0:T(8,128)(2,1)S(1)} collective-permute-done((bf16[16,384]{1,0:T(8,128)(2,1)S(1)}, bf16[16,384]{1,0:T(8,128)(2,1)S(1)}, u32[]{:S(2)}, u32[]{:S(2)}) %collective-permute-start.4) | collective-permute-done | bytes 12320 | tf_op jit(solution)/shard_map/ppermute | solution.py:245
  34.0 3.3 %collective-permute-done = bf16[48,384]{1,0:T(8,128)(2,1)S(1)} collective-permute-done((bf16[48,384]{1,0:T(8,128)(2,1)S(1)}, bf16[48,384]{1,0:T(8,128)(2,1)S(1)}, u32[]{:S(2)}, u32[]{:S(2)}) %collective-permute-start) | collective-permute-done | bytes 36896 | tf_op jit(solution)/shard_map/ppermute | solution.py:255
  37.4 1.9 collective-permute-start.7
  39.5 4.0 %collective-permute-done.7 = bf16[1,64,1152]{2,1,0:T(8,128)(2,1)S(1)} collective-permute-done((bf16[1,64,1152]{2,1,0:T(8,128)(2,1)S(1)}, bf16[1,64,1152]{2,1,0:T(8,128)(2,1)S(1)}, u32[]{:S(2)}, u32[]{:S(2)}) %collective-permute-start.7) | collective-permute-done | bytes 147488 | tf_op jit(solution)/shard_map/ppermute | solution.py:245
  43.5 1.9 collective-permute-start.8
  45.6 15.6 %collective-permute-done.8 = bf16[2,64,1152]{2,1,0:T(8,128)(2,1)S(1)} collective-permute-done((bf16[2,64,1152]{2,1,0:T(8,128)(2,1)S(1)}, bf16[2,64,1152]{2,1,0:T(8,128)(2,1)S(1)}, u32[]{:S(2)}, u32[]{:S(2)}) %collective-permute-start.8) | collective-permute-done | bytes 294944 | tf_op jit(solution)/shard_map/ppermute | solution.py:245
  61.4 2.3 collective-permute-start.9
  67.0 1.8 stack.30.info
  77.5 5.1 %collective-permute-start.22 = (bf16[2,112,384]{2,1,0:T(8,128)(2,1)}, bf16[2,112,384]{2,1,0:T(8,128)(2,1)S(1)}, u32[]{:S(2)}, u32[]{:S(2)}) collective-permute-start(bf16[2,112,384]{2,1,0:T(8,128)(2,1)} %slice.163), channel_id=1, source_target_pairs={{0,8},{1,9},{2,10},{3,11},{4,12},{5,13},{6,14},{7,15},{8,16},{9,17... | collective-permute-start | bytes 516104 | tf_op jit(solution)/shard_map/ppermute | solution.py:245
  82.5 3.0 %collective-permute-start.23 = (bf16[2,112,384]{2,1,0:T(8,128)(2,1)}, bf16[2,112,384]{2,1,0:T(8,128)(2,1)S(1)}, u32[]{:S(2)}, u32[]{:S(2)}) collective-permute-start(bf16[2,112,384]{2,1,0:T(8,128)(2,1)} %slice.163), channel_id=1, source_target_pairs={{0,16},{1,17},{2,18},{3,19},{4,20},{5,21},{6,22},{7,23},{8,24},{9,... | collective-permute-start | bytes 516104 | tf_op jit(solution)/shard_map/ppermute | solution.py:245
  88.1 51.8 %collective-permute-done.17.m1 = bf16[2,112,128]{2,1,0:T(8,128)(2,1)S(1)} collective-permute-done((bf16[2,112,128]{2,1,0:T(8,128)(2,1)S(1)}, bf16[2,112,128]{2,1,0:T(8,128)(2,1)S(1)}, u32[]{:S(2)}, u32[]{:S(2)}) %collective-permute-start.17) | collective-permute-done | bytes 57376 | tf_op jit(solution)/shard_map/ppermute | solution.py:248
  139.9 14.6 %collective-permute-done.18.m3 = bf16[2,112,128]{2,1,0:T(8,128)(2,1)S(1)} collective-permute-done((bf16[2,112,128]{2,1,0:T(8,128)(2,1)S(1)}, bf16[2,112,128]{2,1,0:T(8,128)(2,1)S(1)}, u32[]{:S(2)}, u32[]{:S(2)}) %collective-permute-start.18) | collective-permute-done | bytes 57376 | tf_op jit(solution)/shard_map/ppermute | solution.py:248
  154.5 1.9 next.5
  156.4 1.9 collective-permute-start.19
  158.3 1.9 collective-permute-start.27
  160.2 12.1 %collective-permute-start.20 = (bf16[2,112,128]{2,1,0:T(8,128)(2,1)S(1)}, bf16[2,112,128]{2,1,0:T(8,128)(2,1)S(1)}, u32[]{:S(2)}, u32[]{:S(2)}) collective-permute-start(bf16[2,112,128]{2,1,0:T(8,128)(2,1)S(1)} %get-tuple-element.49), channel_id=1, source_target_pairs={{16,0},{17,1},{18,2},{19,3},{20,4},{21,5},{22,6},{23,7},{24,8},{25... | collective-permute-start | bytes 172040 | tf_op jit(solution)/shard_map/ppermute | solution.py:248
  175.5 3.4 %collective-permute-start.29 = (bf16[4,48,384]{2,1,0:T(8,128)(2,1)S(1)}, bf16[4,48,384]{2,1,0:T(8,128)(2,1)S(1)}, u32[]{:S(2)}, u32[]{:S(2)}) collective-permute-start(bf16[4,48,384]{2,1,0:T(8,128)(2,1)S(1)} %broadcast_select_fusion.2), channel_id=1, source_target_pairs={{0,1},{1,0},{2,3},{3,2},{4,5},{5,4},{6,7},{7,6},{8,9},{9,8},{10,11... | collective-permute-start | bytes 442376 | tf_op jit(solution)/shard_map/ppermute | solution.py:245
  179.0 1.9 collective-permute-start.24
  180.9 4.7 %collective-permute-start.21 = (bf16[2,384,384]{2,1,0:T(8,128)(2,1)S(1)}, bf16[2,384,384]{2,1,0:T(8,128)(2,1)}, u32[]{:S(2)}, u32[]{:S(2)}) collective-permute-start(bf16[2,384,384]{2,1,0:T(8,128)(2,1)S(1)} %get-tuple-element.50.r_ref), channel_id=1, source_target_pairs={{0,128},{128,256},{256,384},{1,129},{129,257},{257,385},{2,130},{1... | collective-permute-start | bytes 1769480 | tf_op jit(solution)/shard_map/ppermute | solution.py:333
  186.3 3.3 %collective-permute-start.30 = (bf16[2,48,384]{2,1,0:T(8,128)(2,1)S(1)}, bf16[2,48,384]{2,1,0:T(8,128)(2,1)S(1)}, u32[]{:S(2)}, u32[]{:S(2)}) collective-permute-start(bf16[2,48,384]{2,1,0:T(8,128)(2,1)S(1)} %broadcast_select_fusion.4), channel_id=1, source_target_pairs={{0,4},{1,5},{2,6},{3,7},{4,0},{5,1},{6,2},{7,3},{8,12},{9,13},{10,... | collective-permute-start | bytes 221192 | tf_op jit(solution)/shard_map/ppermute | solution.py:245
  189.9 2.9 %collective-permute-start.25 = (bf16[2,48,1536]{2,1,0:T(8,128)(2,1)S(1)}, bf16[2,48,1536]{2,1,0:T(8,128)(2,1)S(1)}, u32[]{:S(2)}, u32[]{:S(2)}) collective-permute-start(bf16[2,48,1536]{2,1,0:T(8,128)(2,1)S(1)} %broadcast_select_fusion.1), channel_id=1, source_target_pairs={{0,4},{1,5},{2,6},{3,7},{4,0},{5,1},{6,2},{7,3},{8,12},{9,13},{10,... | collective-permute-start | bytes 884744 | tf_op jit(solution)/shard_map/ppermute | solution.py:245
  192.8 7.3 %collective-permute-done.30 = bf16[2,48,384]{2,1,0:T(8,128)(2,1)S(1)} collective-permute-done((bf16[2,48,384]{2,1,0:T(8,128)(2,1)S(1)}, bf16[2,48,384]{2,1,0:T(8,128)(2,1)S(1)}, u32[]{:S(2)}, u32[]{:S(2)}) %collective-permute-start.30) | collective-permute-done | bytes 73760 | tf_op jit(solution)/shard_map/ppermute | solution.py:245
  200.1 1.9 collective-permute-start.31
  202.1 5.1 %collective-permute-done.25 = bf16[2,48,1536]{2,1,0:T(8,128)(2,1)S(1)} collective-permute-done((bf16[2,48,1536]{2,1,0:T(8,128)(2,1)S(1)}, bf16[2,48,1536]{2,1,0:T(8,128)(2,1)S(1)}, u32[]{:S(2)}, u32[]{:S(2)}) %collective-permute-start.25) | collective-permute-done | bytes 294944 | tf_op jit(solution)/shard_map/ppermute | solution.py:245
  207.3 1.9 collective-permute-start.26
  209.4 4.4 %collective-permute-done.26 = bf16[1,48,1536]{2,1,0:T(8,128)(2,1)S(1)} collective-permute-done((bf16[1,48,1536]{2,1,0:T(8,128)(2,1)S(1)}, bf16[1,48,1536]{2,1,0:T(8,128)(2,1)S(1)}, u32[]{:S(2)}, u32[]{:S(2)}) %collective-permute-start.26) | collective-permute-done | bytes 147488 | tf_op jit(solution)/shard_map/ppermute | solution.py:245
  213.9 9.6 %collective-permute-start.33 = (bf16[48,384]{1,0:T(8,128)(2,1)S(1)}, bf16[48,384]{1,0:T(8,128)(2,1)S(1)}, u32[]{:S(2)}, u32[]{:S(2)}) collective-permute-start(bf16[48,384]{1,0:T(8,128)(2,1)S(1)} %get-tuple-element.55), channel_id=1, source_target_pairs={{16,0},{17,1},{18,2},{19,3},{20,4},{21,5},{22,6},{23,7},{24,8},{25... | collective-permute-start | bytes 110600 | tf_op jit(solution)/shard_map/ppermute | solution.py:245
  223.5 2.6 %collective-permute-start.32 = (bf16[48,768]{1,0:T(8,128)(2,1)S(1)}, bf16[48,768]{1,0:T(8,128)(2,1)S(1)}, u32[]{:S(2)}, u32[]{:S(2)}) collective-permute-start(bf16[48,768]{1,0:T(8,128)(2,1)S(1)} %slice.177), channel_id=1, source_target_pairs={{8,0},{9,1},{10,2},{11,3},{12,4},{13,5},{14,6},{15,7},{16,8},{17,9... | collective-permute-start | bytes 221192 | tf_op jit(solution)/shard_map/ppermute | solution.py:245
  227.3 10.9 %collective-permute-done.32 = bf16[48,768]{1,0:T(8,128)(2,1)S(1)} collective-permute-done((bf16[48,768]{1,0:T(8,128)(2,1)S(1)}, bf16[48,768]{1,0:T(8,128)(2,1)S(1)}, u32[]{:S(2)}, u32[]{:S(2)}) %collective-permute-start.32) | collective-permute-done | bytes 73760 | tf_op jit(solution)/shard_map/ppermute | solution.py:245
  (103 shorter events, 27.1 us)
Async XLA Ops:
  1.5 22.3 %collective-permute-start.2 = (bf16[16,384]{1,0:T(8,128)(2,1)S(1)}, bf16[16,384]{1,0:T(8,128)(2,1)S(1)}, u32[]{:S(2)}, u32[]{:S(2)}) collective-permute-start(bf16[16,384]{1,0:T(8,128)(2,1)S(1)} %slice.158), channel_id=1, source_target_pairs={{0,16},{1,19},{2,22},{8,24},{9,27},{10,30},{16,32},{17,35},{18,38}... | collective-permute-start | bytes 36872 | tf_op jit(solution)/shard_map/ppermute | solution.py:245
  16.6 17.4 %collective-permute-start.1 = (bf16[16,768]{1,0:T(8,128)(2,1)S(1)}, bf16[16,768]{1,0:T(8,128)(2,1)S(1)}, u32[]{:S(2)}, u32[]{:S(2)}) collective-permute-start(bf16[16,768]{1,0:T(8,128)(2,1)S(1)} %slice.157), channel_id=1, source_target_pairs={{0,8},{1,11},{2,14},{8,16},{9,19},{10,22},{16,24},{17,27},{18,30},... | collective-permute-start | bytes 73736 | tf_op jit(solution)/shard_map/ppermute | solution.py:245
  17.9 14.8 %collective-permute-start.4 = (bf16[16,384]{1,0:T(8,128)(2,1)S(1)}, bf16[16,384]{1,0:T(8,128)(2,1)S(1)}, u32[]{:S(2)}, u32[]{:S(2)}) collective-permute-start(bf16[16,384]{1,0:T(8,128)(2,1)S(1)} %slice.160), channel_id=1, source_target_pairs={{0,17},{1,20},{2,23},{8,25},{9,28},{10,31},{16,33},{17,36},{18,39}... | collective-permute-start | bytes 36872 | tf_op jit(solution)/shard_map/ppermute | solution.py:245
  19.8 14.2 %collective-permute-start.3 = (bf16[16,768]{1,0:T(8,128)(2,1)S(1)}, bf16[16,768]{1,0:T(8,128)(2,1)S(1)}, u32[]{:S(2)}, u32[]{:S(2)}) collective-permute-start(bf16[16,768]{1,0:T(8,128)(2,1)S(1)} %slice.159), channel_id=1, source_target_pairs={{0,9},{1,12},{2,15},{8,17},{9,20},{10,23},{16,25},{17,28},{18,31},... | collective-permute-start | bytes 73736 | tf_op jit(solution)/shard_map/ppermute | solution.py:245
  21.8 12.2 %collective-permute-start.6 = (bf16[16,384]{1,0:T(8,128)(2,1)S(1)}, bf16[16,384]{1,0:T(8,128)(2,1)S(1)}, u32[]{:S(2)}, u32[]{:S(2)}) collective-permute-start(bf16[16,384]{1,0:T(8,128)(2,1)S(1)} %slice.162), channel_id=1, source_target_pairs={{0,18},{1,21},{8,26},{9,29},{16,34},{17,37},{24,42},{25,45},{32,50... | collective-permute-start | bytes 36872 | tf_op jit(solution)/shard_map/ppermute | solution.py:245
  23.8 10.2 %collective-permute-start.5 = (bf16[16,768]{1,0:T(8,128)(2,1)S(1)}, bf16[16,768]{1,0:T(8,128)(2,1)S(1)}, u32[]{:S(2)}, u32[]{:S(2)}) collective-permute-start(bf16[16,768]{1,0:T(8,128)(2,1)S(1)} %slice.161), channel_id=1, source_target_pairs={{0,10},{1,13},{8,18},{9,21},{16,26},{17,29},{24,34},{25,37},{32,42... | collective-permute-start | bytes 73736 | tf_op jit(solution)/shard_map/ppermute | solution.py:245
  32.7 4.7 %collective-permute-start = (bf16[48,384]{1,0:T(8,128)(2,1)S(1)}, bf16[48,384]{1,0:T(8,128)(2,1)S(1)}, u32[]{:S(2)}, u32[]{:S(2)}) collective-permute-start(bf16[48,384]{1,0:T(8,128)(2,1)S(1)} %pad_maximum_fusion), channel_id=1, source_target_pairs={{128,0},{256,128},{384,256},{129,1},{257,129},{385,257},{130,2},{2... | collective-permute-start | bytes 110600 | tf_op jit(solution)/shard_map/ppermute | solution.py:255
  37.4 6.1 %collective-permute-start.7 = (bf16[1,64,1152]{2,1,0:T(8,128)(2,1)S(1)}, bf16[1,64,1152]{2,1,0:T(8,128)(2,1)S(1)}, u32[]{:S(2)}, u32[]{:S(2)}) collective-permute-start(bf16[1,64,1152]{2,1,0:T(8,128)(2,1)S(1)} %maximum_bitcast_fusion), channel_id=1, source_target_pairs={{0,2},{1,3},{2,0},{3,1},{4,6},{5,7},{6,4},{7,5},{8,10},{9,11},{10,... | collective-permute-start | bytes 442376 | tf_op jit(solution)/shard_map/ppermute | solution.py:245
  43.5 17.7 %collective-permute-start.8 = (bf16[2,64,1152]{2,1,0:T(8,128)(2,1)S(1)}, bf16[2,64,1152]{2,1,0:T(8,128)(2,1)S(1)}, u32[]{:S(2)}, u32[]{:S(2)}) collective-permute-start(bf16[2,64,1152]{2,1,0:T(8,128)(2,1)S(1)} %maximum_select_fusion.3), channel_id=1, source_target_pairs={{0,4},{1,5},{2,6},{3,7},{4,0},{5,1},{6,2},{7,3},{8,12},{9,13},{10,... | collective-permute-start | bytes 884744 | tf_op jit(solution)/shard_map/ppermute | solution.py:245
  61.4 7.6 %collective-permute-start.9 = (bf16[4,64,1152]{2,1,0:T(8,128)(2,1)S(1)}, bf16[4,64,1152]{2,1,0:T(8,128)(2,1)S(1)}, u32[]{:S(2)}, u32[]{:S(2)}) collective-permute-start(bf16[4,64,1152]{2,1,0:T(8,128)(2,1)S(1)} %maximum_select_fusion.1), channel_id=1, source_target_pairs={{0,1},{1,0},{2,3},{3,2},{4,5},{5,4},{6,7},{7,6},{8,9},{9,8},{10,11... | collective-permute-start | bytes 1769480 | tf_op jit(solution)/shard_map/ppermute | solution.py:245
  70.8 2.1 collective-permute-start.10
  71.5 1.3 collective-permute-start.11
  73.5 2.1 collective-permute-start.13
  74.2 1.3 collective-permute-start.14
  76.2 78.4 %collective-permute-start.16 = (bf16[2,384,384]{2,1,0:T(8,128)(2,1)S(1)}, bf16[2,384,384]{2,1,0:T(8,128)(2,1)S(1)}, u32[]{:S(2)}, u32[]{:S(2)}) collective-permute-start(bf16[2,384,384]{2,1,0:T(8,128)(2,1)S(1)} %get-tuple-element.41), channel_id=1, source_target_pairs={{128,0},{129,1},{130,2},{131,3},{132,4},{133,5},{134,6},{135,7},{1... | collective-permute-start | bytes 1769480 | tf_op jit(solution)/shard_map/ppermute | solution.py:248
  77.5 94.9 %collective-permute-start.22 = (bf16[2,112,384]{2,1,0:T(8,128)(2,1)}, bf16[2,112,384]{2,1,0:T(8,128)(2,1)S(1)}, u32[]{:S(2)}, u32[]{:S(2)}) collective-permute-start(bf16[2,112,384]{2,1,0:T(8,128)(2,1)} %slice.163), channel_id=1, source_target_pairs={{0,8},{1,9},{2,10},{3,11},{4,12},{5,13},{6,14},{7,15},{8,16},{9,17... | collective-permute-start | bytes 516104 | tf_op jit(solution)/shard_map/ppermute | solution.py:245
  82.5 91.1 %collective-permute-start.23 = (bf16[2,112,384]{2,1,0:T(8,128)(2,1)}, bf16[2,112,384]{2,1,0:T(8,128)(2,1)S(1)}, u32[]{:S(2)}, u32[]{:S(2)}) collective-permute-start(bf16[2,112,384]{2,1,0:T(8,128)(2,1)} %slice.163), channel_id=1, source_target_pairs={{0,16},{1,17},{2,18},{3,19},{4,20},{5,21},{6,22},{7,23},{8,24},{9,... | collective-permute-start | bytes 516104 | tf_op jit(solution)/shard_map/ppermute | solution.py:245
  85.5 54.4 %collective-permute-start.17 = (bf16[2,112,128]{2,1,0:T(8,128)(2,1)S(1)}, bf16[2,112,128]{2,1,0:T(8,128)(2,1)S(1)}, u32[]{:S(2)}, u32[]{:S(2)}) collective-permute-start(bf16[2,112,128]{2,1,0:T(8,128)(2,1)S(1)} %get-tuple-element.42), channel_id=1, source_target_pairs={{136,0},{137,1},{138,2},{139,3},{140,4},{141,5},{142,6},{143,7},{1... | collective-permute-start | bytes 172040 | tf_op jit(solution)/shard_map/ppermute | solution.py:248
  86.8 67.7 %collective-permute-start.18 = (bf16[2,112,128]{2,1,0:T(8,128)(2,1)S(1)}, bf16[2,112,128]{2,1,0:T(8,128)(2,1)S(1)}, u32[]{:S(2)}, u32[]{:S(2)}) collective-permute-start(bf16[2,112,128]{2,1,0:T(8,128)(2,1)S(1)} %get-tuple-element.43), channel_id=1, source_target_pairs={{144,0},{145,1},{146,2},{147,3},{148,4},{149,5},{150,6},{151,7},{1... | collective-permute-start | bytes 172040 | tf_op jit(solution)/shard_map/ppermute | solution.py:248
  156.4 18.4 %collective-permute-start.19 = (bf16[2,112,128]{2,1,0:T(8,128)(2,1)}, bf16[2,112,128]{2,1,0:T(8,128)(2,1)S(1)}, u32[]{:S(2)}, u32[]{:S(2)}) collective-permute-start(bf16[2,112,128]{2,1,0:T(8,128)(2,1)} %get-tuple-element.48), channel_id=1, source_target_pairs={{8,0},{9,1},{10,2},{11,3},{12,4},{13,5},{14,6},{15,7},{16,8},{17,9... | collective-permute-start | bytes 172040 | tf_op jit(solution)/shard_map/ppermute | solution.py:248
  158.3 16.5 %collective-permute-start.27 = (bf16[2,112,128]{2,1,0:T(8,128)(2,1)S(1)}, bf16[2,112,128]{2,1,0:T(8,128)(2,1)}, u32[]{:S(2)}, u32[]{:S(2)}) collective-permute-start(bf16[2,112,128]{2,1,0:T(8,128)(2,1)S(1)} %get-tuple-element.52), channel_id=1, source_target_pairs={{0,128},{128,256},{256,384},{1,129},{129,257},{257,385},{2,130},{1... | collective-permute-start | bytes 172040 | tf_op jit(solution)/shard_map/ppermute | solution.py:334
  160.2 14.6 %collective-permute-start.20 = (bf16[2,112,128]{2,1,0:T(8,128)(2,1)S(1)}, bf16[2,112,128]{2,1,0:T(8,128)(2,1)S(1)}, u32[]{:S(2)}, u32[]{:S(2)}) collective-permute-start(bf16[2,112,128]{2,1,0:T(8,128)(2,1)S(1)} %get-tuple-element.49), channel_id=1, source_target_pairs={{16,0},{17,1},{18,2},{19,3},{20,4},{21,5},{22,6},{23,7},{24,8},{25... | collective-permute-start | bytes 172040 | tf_op jit(solution)/shard_map/ppermute | solution.py:248
  172.3 2.5 %collective-permute-start.28 = (bf16[2,112,128]{2,1,0:T(8,128)(2,1)S(1)}, bf16[2,112,128]{2,1,0:T(8,128)(2,1)S(1)}, u32[]{:S(2)}, u32[]{:S(2)}) collective-permute-start(bf16[2,112,128]{2,1,0:T(8,128)(2,1)S(1)} %get-tuple-element.53), channel_id=1, source_target_pairs={{0,128},{128,256},{256,384},{1,129},{129,257},{257,385},{2,130},{1... | collective-permute-start | bytes 172040 | tf_op jit(solution)/shard_map/ppermute | solution.py:335
  175.5 10.7 %collective-permute-start.29 = (bf16[4,48,384]{2,1,0:T(8,128)(2,1)S(1)}, bf16[4,48,384]{2,1,0:T(8,128)(2,1)S(1)}, u32[]{:S(2)}, u32[]{:S(2)}) collective-permute-start(bf16[4,48,384]{2,1,0:T(8,128)(2,1)S(1)} %broadcast_select_fusion.2), channel_id=1, source_target_pairs={{0,1},{1,0},{2,3},{3,2},{4,5},{5,4},{6,7},{7,6},{8,9},{9,8},{10,11... | collective-permute-start | bytes 442376 | tf_op jit(solution)/shard_map/ppermute | solution.py:245
  179.0 10.6 %collective-permute-start.24 = (bf16[4,48,1536]{2,1,0:T(8,128)(2,1)S(1)}, bf16[4,48,1536]{2,1,0:T(8,128)(2,1)S(1)}, u32[]{:S(2)}, u32[]{:S(2)}) collective-permute-start(bf16[4,48,1536]{2,1,0:T(8,128)(2,1)S(1)} %broadcast_select_fusion), channel_id=1, source_target_pairs={{0,1},{1,0},{2,3},{3,2},{4,5},{5,4},{6,7},{7,6},{8,9},{9,8},{10,11... | collective-permute-start | bytes 1769480 | tf_op jit(solution)/shard_map/ppermute | solution.py:245
  180.9 45.2 %collective-permute-start.21 = (bf16[2,384,384]{2,1,0:T(8,128)(2,1)S(1)}, bf16[2,384,384]{2,1,0:T(8,128)(2,1)}, u32[]{:S(2)}, u32[]{:S(2)}) collective-permute-start(bf16[2,384,384]{2,1,0:T(8,128)(2,1)S(1)} %get-tuple-element.50.r_ref), channel_id=1, source_target_pairs={{0,128},{128,256},{256,384},{1,129},{129,257},{257,385},{2,130},{1... | collective-permute-start | bytes 1769480 | tf_op jit(solution)/shard_map/ppermute | solution.py:333
  186.3 13.8 %collective-permute-start.30 = (bf16[2,48,384]{2,1,0:T(8,128)(2,1)S(1)}, bf16[2,48,384]{2,1,0:T(8,128)(2,1)S(1)}, u32[]{:S(2)}, u32[]{:S(2)}) collective-permute-start(bf16[2,48,384]{2,1,0:T(8,128)(2,1)S(1)} %broadcast_select_fusion.4), channel_id=1, source_target_pairs={{0,4},{1,5},{2,6},{3,7},{4,0},{5,1},{6,2},{7,3},{8,12},{9,13},{10,... | collective-permute-start | bytes 221192 | tf_op jit(solution)/shard_map/ppermute | solution.py:245
  189.9 17.3 %collective-permute-start.25 = (bf16[2,48,1536]{2,1,0:T(8,128)(2,1)S(1)}, bf16[2,48,1536]{2,1,0:T(8,128)(2,1)S(1)}, u32[]{:S(2)}, u32[]{:S(2)}) collective-permute-start(bf16[2,48,1536]{2,1,0:T(8,128)(2,1)S(1)} %broadcast_select_fusion.1), channel_id=1, source_target_pairs={{0,4},{1,5},{2,6},{3,7},{4,0},{5,1},{6,2},{7,3},{8,12},{9,13},{10,... | collective-permute-start | bytes 884744 | tf_op jit(solution)/shard_map/ppermute | solution.py:245
  200.1 9.1 %collective-permute-start.31 = (bf16[1,48,384]{2,1,0:T(8,128)(2,1)S(1)}, bf16[1,48,384]{2,1,0:T(8,128)(2,1)S(1)}, u32[]{:S(2)}, u32[]{:S(2)}) collective-permute-start(bf16[1,48,384]{2,1,0:T(8,128)(2,1)S(1)} %broadcast_select_fusion.7), channel_id=1, source_target_pairs={{0,2},{1,3},{2,0},{3,1},{4,6},{5,7},{6,4},{7,5},{8,10},{9,11},{10,... | collective-permute-start | bytes 110600 | tf_op jit(solution)/shard_map/ppermute | solution.py:245
  207.3 6.4 %collective-permute-start.26 = (bf16[1,48,1536]{2,1,0:T(8,128)(2,1)S(1)}, bf16[1,48,1536]{2,1,0:T(8,128)(2,1)S(1)}, u32[]{:S(2)}, u32[]{:S(2)}) collective-permute-start(bf16[1,48,1536]{2,1,0:T(8,128)(2,1)S(1)} %broadcast_select_fusion.3), channel_id=1, source_target_pairs={{0,2},{1,3},{2,0},{3,1},{4,6},{5,7},{6,4},{7,5},{8,10},{9,11},{10,... | collective-permute-start | bytes 442376 | tf_op jit(solution)/shard_map/ppermute | solution.py:245
  213.9 13.4 %collective-permute-start.33 = (bf16[48,384]{1,0:T(8,128)(2,1)S(1)}, bf16[48,384]{1,0:T(8,128)(2,1)S(1)}, u32[]{:S(2)}, u32[]{:S(2)}) collective-permute-start(bf16[48,384]{1,0:T(8,128)(2,1)S(1)} %get-tuple-element.55), channel_id=1, source_target_pairs={{16,0},{17,1},{18,2},{19,3},{20,4},{21,5},{22,6},{23,7},{24,8},{25... | collective-permute-start | bytes 110600 | tf_op jit(solution)/shard_map/ppermute | solution.py:245
  223.5 14.7 %collective-permute-start.32 = (bf16[48,768]{1,0:T(8,128)(2,1)S(1)}, bf16[48,768]{1,0:T(8,128)(2,1)S(1)}, u32[]{:S(2)}, u32[]{:S(2)}) collective-permute-start(bf16[48,768]{1,0:T(8,128)(2,1)S(1)} %slice.177), channel_id=1, source_target_pairs={{8,0},{9,1},{10,2},{11,3},{12,4},{13,5},{14,6},{15,7},{16,8},{17,9... | collective-permute-start | bytes 221192 | tf_op jit(solution)/shard_map/ppermute | solution.py:245
  (7 other events, 171.3 us)
